TPU v7x, 32 devices: a whole 2x2x4 slice. The times are simulated.
32 devices in a mesh: groups: 2 (over y), frame: 4 (over z), panel: 2 (over x), sub: 2 (over core).
Axes of the slice: x: 2, y: 2, z: 4, core: 2. Of those that a mesh axis runs over, the one named last changes fastest.
Arguments:
- frames: bfloat16 [2048, 65536], P(('groups', 'frame'), ('panel', 'sub')), parts along dimension 0, may hold values from -16 to 16
- slices: float32 [32, 65536], P(('groups', 'frame'), ('panel', 'sub')), parts along dimension 0, may hold values from -8 to 8
- log_prior: float32 [4096], replicated, may hold values from -2 to 2
- orient: int32 [32], P('groups'), parts along dimension 0, may hold values from 0 to 4095
Outputs:
- new_slices: float32 [32, 65536], P(('groups', 'frame'), ('panel', 'sub')), parts along dimension 0
There are 2 independent parts, one for each index of `groups`. A program takes and returns all parts, laid end to end along the dimension named above; an argument that names none is the same for every part. Nothing has to cross between parts.
All inputs are finite; a program needn't handle non-finite values.
Results may differ from a plain program's by a relative error of at most 0.022.
The roundings to bfloat16 on the way count: a program that leaves them out, or rounds other values in their place, can miss the bound.
Values may be sent and summed in bfloat16 or wider, within the bound.
A program may use at most 64 MiB of HBM per device.

v0:
```python
import math
import jax
import jax.numpy as jnp
from jax import lax
from jax.sharding import PartitionSpec as P

PIX = 65536
ITERS = 2


def fetch_slices(owned_b):
    return lax.all_gather(owned_b, "frame", axis=0, tiled=True)


def owner_update(weights, frames, counts, owned_b, offset):
    owned = owned_b.shape[0]
    mine = lax.psum_scatter(
        jnp.einsum("fm,fp->mp", weights, frames, preferred_element_type=jnp.float32).astype(
            jnp.bfloat16
        ),
        "frame",
        scatter_dimension=0,
        tiled=True,
    ).astype(jnp.float32)
    my_counts = lax.dynamic_slice_in_dim(counts, offset, owned, 0)
    return (mine + owned_b.astype(jnp.float32)) / (my_counts + 1.0)[:, None]


def local(frames, slices, log_prior, orient):
    owned = slices.shape[0]
    temper = 3.0 / math.sqrt(PIX)
    matches = orient[:, None] == jnp.arange(log_prior.shape[0], dtype=jnp.int32)[None, :]
    prior = jnp.sum(jnp.where(matches, log_prior[None, :], 0.0), axis=1)
    offset = lax.axis_index("frame") * owned
    current = slices
    owned_b = slices.astype(jnp.bfloat16)
    for step in range(ITERS):
        if step == 0:
            gathered = fetch_slices(owned_b)
        else:
            gathered = fetch_slices(owned_b)
        wide = gathered.astype(jnp.float32)
        norms = jnp.sum(wide * wide, axis=1)
        raw = (
            jnp.einsum("fp,mp->fm", frames, gathered, preferred_element_type=jnp.float32)
            - 0.5 * norms[None, :]
        )
        summed = lax.psum(raw, ("panel", "sub"))
        weights = jax.nn.softmax(temper * summed + prior[None, :], axis=1).astype(jnp.bfloat16)
        counts = lax.psum(jnp.sum(weights.astype(jnp.float32), axis=0), "frame")
        if step + 1 < ITERS:
            current = owner_update(weights, frames, counts, owned_b, offset)
            owned_b = current.astype(jnp.bfloat16)
        else:
            current = owner_update(weights, frames, counts, owned_b, offset)
    return current


def solution(mesh):
    in_specs = (
        P(("groups", "frame"), ("panel", "sub")),
        P(("groups", "frame"), ("panel", "sub")),
        P(),
        P("groups"),
    )
    out_specs = P(("groups", "frame"), ("panel", "sub"))
    return jax.shard_map(local, mesh=mesh, in_specs=in_specs, out_specs=out_specs, check_vma=False)
```

profile of v0, /device:TPU:0, one launch (start us, length us, event | category | flops | bytes accessed | tf_op | source)
XLA Modules:
  0.0 173.9 jit_solution(4613914813418080331)
XLA Ops:
  6.5 0.0 copy-start.2
  6.5 0.0 copy-start.1
  6.5 0.0 all-reduce.5.cloned.1.call-start
  6.5 1.0 convert_bitcast_fusion
  7.6 17.4 %all-gather = bf16[4,4,16384]{2,1,0:T(4,128)(2,1)S(1)} all-gather(bf16[1,4,16384]{2,1,0:T(4,128)(2,1)S(1)} %convert_bitcast_fusion), channel_id=1, replica_groups=mesh['groups'=2,'frame'=4,'panel'=2,'sub'=2] {'frame'}, dimensions={0}, use_global_device_ids=true | all-gather | bytes 655360 | tf_op jit(solution)/shard_map/all_gather | solution.py:12
  24.9 0.1 reshape.18
  25.1 0.2 multiply_reduce_fusion.1
  25.3 0.0 copy-start.3
  25.3 0.0 copy-start
  25.3 5.7 %convolution_subtract_fusion.1 = f32[256,16]{0,1:T(8,128)S(1)} fusion(bf16[256,16384]{1,0:T(8,128)(2,1)} %param.4, bf16[16,16384]{1,0:T(8,128)(2,1)S(1)} %reshape.18, f32[16]{0:T(128)S(1)} %broadcast_multiply_fusion.1), kind=kOutput, calls=%fused_computation.4 | convolution fusion | flops 134221824 | bytes 8929344 | tf_op jit(solution)/shard_map/fp,mp->fm/dot_general | solution.py:45
  31.0 10.1 %psum.28 = f32[256,16]{0,1:T(8,128)S(1)} all-reduce(f32[256,16]{0,1:T(8,128)S(1)} %convolution_subtract_fusion.1), channel_id=1, replica_groups=mesh['groups'=2,'frame'=4,'panel'=2,'sub'=2] {'panel','sub'}, use_global_device_ids=true, to_apply=%region_1.2 | all-reduce | flops 4096 | bytes 32768 | tf_op jit(solution)/shard_map/psum | solution.py:48
  41.1 0.0 copy-done.2
  41.1 0.0 copy-done.1
  41.1 0.2 select_reduce_fusion
  41.4 0.1 fusion.2
  41.5 0.1 fusion.4
  41.6 0.2 convert_reduce_fusion.1
  41.7 5.4 %convolution_convert_fusion.1 = bf16[16,16384]{1,0:T(8,128)(2,1)} fusion(bf16[256,16]{0,1:T(8,128)(2,1)S(1)} %get-tuple-element.8, bf16[256,16384]{1,0:T(8,128)(2,1)} %param.4), kind=kOutput, calls=%fused_computation.1 | convolution fusion | flops 134479872 | bytes 8921088 | tf_op jit(solution)/shard_map/fm,fp->mp/dot_general | solution.py:18
  47.2 0.0 all-reduce.5.cloned.1.call-update
  47.2 0.0 all-reduce.7.cloned.1.call-start
  47.2 0.0 copy-done.3
  47.3 0.6 dynamic-slice
  48.5 12.6 %psum.29 = f32[16]{0:T(128)S(1)} all-reduce(f32[16]{0:T(128)S(1)} %get-tuple-element.7), channel_id=1, replica_groups=mesh['groups'=2,'frame'=4,'panel'=2,'sub'=2] {'frame'}, use_global_device_ids=true, to_apply=%region_7.8 | all-reduce | flops 16 | bytes 128 | tf_op jit(solution)/shard_map/psum | solution.py:50
  61.0 0.1 dynamic-slice_add_fusion.1
  61.1 26.4 %all-reduce.5.cloned.1.call-done = bf16[16,16384]{1,0:T(8,128)(2,1)} async-done(((bf16[16,16384]{1,0:T(8,128)(2,1)}), bf16[16,16384]{1,0:T(8,128)(2,1)}) %all-reduce.5.cloned.1.call-update) | async-done | bytes 524304
  87.6 0.0 copy-done
  87.6 1.1 fusion.1
  88.6 16.2 %all-gather.1 = bf16[4,4,16384]{2,1,0:T(4,128)(2,1)S(1)} all-gather(bf16[1,4,16384]{2,1,0:T(4,128)(2,1)S(1)} %bitcast.14), channel_id=1, replica_groups=mesh['groups'=2,'frame'=4,'panel'=2,'sub'=2] {'frame'}, dimensions={0}, use_global_device_ids=true | all-gather | bytes 655360 | tf_op jit(solution)/shard_map/all_gather | solution.py:12
  104.8 0.1 reshape.20
  104.9 0.2 multiply_reduce_fusion
  105.2 5.6 %fusion = f32[256,16]{0,1:T(8,128)S(1)} fusion(bf16[16,16384]{1,0:T(8,128)(2,1)S(1)} %reshape.20, bf16[256,16384]{1,0:T(8,128)(2,1)} %param.4, f32[16]{0:T(128)S(1)} %broadcast_multiply_fusion), kind=kOutput, calls=%fused_computation.3 | convolution fusion | flops 134221824 | bytes 8929344 | tf_op jit(solution)/shard_map/fp,mp->fm/dot_general | solution.py:45
  110.8 10.1 %psum.30 = f32[256,16]{0,1:T(8,128)S(1)} all-reduce(f32[256,16]{0,1:T(8,128)S(1)} %fusion), channel_id=1, replica_groups=mesh['groups'=2,'frame'=4,'panel'=2,'sub'=2] {'panel','sub'}, use_global_device_ids=true, to_apply=%region_9.10 | all-reduce | flops 4096 | bytes 32768 | tf_op jit(solution)/shard_map/psum | solution.py:48
  120.9 0.1 fusion.3
  121.0 0.1 fusion.5
  121.1 0.2 convert_reduce_fusion
  121.3 5.4 %convolution_convert_fusion = bf16[16,16384]{1,0:T(8,128)(2,1)} fusion(bf16[256,16]{0,1:T(8,128)(2,1)S(1)} %get-tuple-element.6, bf16[256,16384]{1,0:T(8,128)(2,1)} %param.4), kind=kOutput, calls=%fused_computation | convolution fusion | flops 134479872 | bytes 8921088 | tf_op jit(solution)/shard_map/fm,fp->mp/dot_general | solution.py:18
  126.7 0.0 all-reduce.7.cloned.1.call-update
  126.7 10.8 %psum.31 = f32[16]{0:T(128)S(1)} all-reduce(f32[16]{0:T(128)S(1)} %get-tuple-element.5), channel_id=1, replica_groups=mesh['groups'=2,'frame'=4,'panel'=2,'sub'=2] {'frame'}, use_global_device_ids=true, to_apply=%region_14.15 | all-reduce | flops 16 | bytes 128 | tf_op jit(solution)/shard_map/psum | solution.py:50
  137.5 0.1 dynamic-slice_add_fusion
  137.6 27.7 %all-reduce.7.cloned.1.call-done = bf16[16,16384]{1,0:T(8,128)(2,1)} async-done(((bf16[16,16384]{1,0:T(8,128)(2,1)}), bf16[16,16384]{1,0:T(8,128)(2,1)}) %all-reduce.7.cloned.1.call-update) | async-done | bytes 524304
  165.3 1.8 %add_divide_fusion = f32[4,16384]{1,0:T(4,128)} fusion(bf16[4,16384]{1,0:T(4,128)(2,1)S(1)} %fusion.1, bf16[16,16384]{1,0:T(8,128)(2,1)} %all-reduce.7.cloned.1.call-done, u32[]{:T(128)S(6)} %multiply.1, f32[4]{0:T(128)S(1)} %dynamic-slice_add_fusion), kind=kLoop, calls=%fused_computation.7 | loop fusion | flops 262144 | bytes 524308 | tf_op jit(solution)/shard_map/div | solution.py:26
  (2 shorter events, 0.0 us)
Async XLA Ops:
  6.5 34.6 %copy-start.2 = (s32[16]{0:T(128)S(1)}, s32[16]{0:T(128)}, u32[]{:S(2)}) copy-start(s32[16]{0:T(128)} %param.7) | copy-start | bytes 196
  6.5 34.6 %copy-start.1 = (f32[4096]{0:T(1024)S(1)}, f32[4096]{0:T(1024)}, u32[]{:S(2)}) copy-start(f32[4096]{0:T(1024)} %param.6) | copy-start | bytes 49156
  6.5 81.0 %all-reduce.5.cloned.1.call-start = ((), (), s32[]{:S(2)}) async-start(), calls=%async_computation | async-start | bytes 1048576
  25.3 21.9 %copy-start.3 = (u32[32]{0:T(128)S(1)}, u32[32]{0:T(128)}, u32[]{:S(2)}) copy-start(u32[32]{0:T(128)} %constant.25) | copy-start | bytes 388
  25.3 62.2 %copy-start = (f32[4,16384]{1,0:T(4,128)S(1)}, f32[4,16384]{1,0:T(4,128)}, u32[]{:S(2)}) copy-start(f32[4,16384]{1,0:T(4,128)} %param.5) | copy-start | bytes 786436
  47.2 118.2 %all-reduce.7.cloned.1.call-start = ((), (), s32[]{:S(2)}) async-start(), calls=%async_computation.1 | async-start | bytes 1048576
Sparse Core Ops, SparseCore 0:
  47.3 40.1 all-reduce.4
  126.9 38.4 all-reduce.6
where the time goes:
time: 174 us
  blocking collectives  77.1 us (44%)
  waiting for transfers between devices  54.2 us (31%)
  matrix products  22.2 us (13%)
  between operations  14.1 us (8%)
  other arithmetic  5.48 us (3%)
    unnamed x4, waiting for transfers between devices  54.2 us
    all_gather x2, blocking collectives, fetch_slices(): return lax.all_gather(owned_b, 'frame', axis=0, tiled=True)  33.5 us
    psum x2, blocking collectives, local(): counts = lax.psum(jnp.sum(weights.astype(jnp.float32), axis=0), 'frame')  23.3 us
    psum x2, blocking collectives, local(): summed = lax.psum(raw, ('panel', 'sub'))  20.2 us
    dot_general x2, matrix products, local(): jnp.einsum('fp,mp->fm', frames, gathered, preferred_element_type=jnp.floa...  11.3 us
    dot_general x2, matrix products, owner_update(): jnp.einsum('fm,fp->mp', weights, frames, preferred_element_type=jnp.float32)  10.8 us
  transfers between devices with their start and end apart: 2, of which 2 were waited for; matrix products, arithmetic and copies ran while one was open for 0% of the time, Pallas kernels for 0%

commit v1 on v0

--- a/solution.py
+++ b/solution.py
@@ -9,7 +9,35 @@
 
 
 def fetch_slices(owned_b):
-    return lax.all_gather(owned_b, "frame", axis=0, tiled=True)
+
+    def mark_the_classes(own_rows):
+        last, v_next, g_now = (lax.axis_size("frame"), lax.axis_index("frame"), own_rows.shape[0])
+        history = []
+        for it, src_i in enumerate(own_rows.shape):
+            history.append(src_i * last if it == 0 else src_i)
+        y_new = lax.dynamic_update_slice_in_dim(
+            jnp.zeros(history, own_rows.dtype), own_rows, v_next * g_now, axis=0
+        )
+        passed = p_next = own_rows
+        for at in [*range(1, last // 2 + 1)]:
+            column = []
+            for it in [*range(last)]:
+                column.append((it, (it + 1) % last))
+            passed = lax.ppermute(passed, "frame", column)
+            y_new = lax.dynamic_update_slice_in_dim(
+                y_new, passed, (v_next - at) % last * g_now, axis=0
+            )
+            if 2 * at < last:
+                rack = []
+                for it in [*range(last)]:
+                    rack.append((it, (it - 1) % last))
+                p_next = lax.ppermute(p_next, "frame", rack)
+                y_new = lax.dynamic_update_slice_in_dim(
+                    y_new, p_next, (v_next + at) % last * g_now, axis=0
+                )
+        return y_new
+
+    return mark_the_classes(owned_b)
 
 
 def owner_update(weights, frames, counts, owned_b, offset):

time: 174 us -> 167 us (0.960)
  blocking collectives: 77.1 us -> 39.6 us
  waiting for transfers between devices: 54.2 us -> 74 us
  starting transfers between devices: 0.04 us -> 9.57 us
    all_gather x2 -> x0, blocking collectives: 33.5 us -> none  [fetch_slices(): return lax.all_gather(owned_b, 'frame', axis=0, tiled=True)]
    ppermute x0 -> x6, waiting for transfers between devices: none -> 19.8 us  [the longest x4 18.5 us: mark_the_classes(): passed = lax.ppermute(passed, 'frame', column)]
    ppermute x0 -> x6, starting transfers between devices: none -> 9.53 us  [the longest x4 4.88 us: mark_the_classes(): passed = lax.ppermute(passed, 'frame', column)]
    psum x2, blocking collectives: 23.3 us -> 19.3 us  [local(): counts = lax.psum(jnp.sum(weights.astype(jnp.float32), axis=0), 'frame')]
    dynamic_update_slice x0 -> x2, other arithmetic: none -> 2.23 us  [mark_the_classes(): lax.dynamic_update_slice_in_dim(jnp.zeros(history, own_rows.dtype), own_r...]
  transfers between devices with their start and end apart: 2 -> 8, of which waited for: 2 -> 7; matrix products, arithmetic and copies ran while one was open for 0% -> 1% of each run, Pallas kernels for 0% -> 0%
where the time goes in v1:
time: 167 us
  waiting for transfers between devices  74 us (44%)
  blocking collectives  39.6 us (24%)
  matrix products  22.1 us (13%)
  between operations  14.1 us (8%)
  starting transfers between devices  9.57 us (6%)
  other arithmetic  6.33 us (4%)
    unnamed x4, waiting for transfers between devices  54.2 us
    psum x2, blocking collectives, local(): summed = lax.psum(raw, ('panel', 'sub'))  20.2 us
    psum x2, blocking collectives, local(): counts = lax.psum(jnp.sum(weights.astype(jnp.float32), axis=0), 'frame')  19.3 us
    ppermute x4, waiting for transfers between devices, mark_the_classes(): passed = lax.ppermute(passed, 'frame', column)  18.5 us
    dot_general x2, matrix products, local(): jnp.einsum('fp,mp->fm', frames, gathered, preferred_element_type=jnp.floa...  11.3 us
    dot_general x2, matrix products, owner_update(): jnp.einsum('fm,fp->mp', weights, frames, preferred_element_type=jnp.float32)  10.8 us
    ppermute x4, starting transfers between devices, mark_the_classes(): passed = lax.ppermute(passed, 'frame', column)  4.88 us
    ppermute x2, starting transfers between devices, mark_the_classes(): p_next = lax.ppermute(p_next, 'frame', rack)  4.65 us
  transfers between devices with their start and end apart: 8, of which 7 were waited for; matrix products, arithmetic and copies ran while one was open for 1% of the time, Pallas kernels for 0%

profile of v1, /device:TPU:0, one launch (start us, length us, event | category | flops | bytes accessed | tf_op | source)
XLA Modules:
  0.0 166.9 jit_solution(11557339152969574369)
XLA Ops:
  6.5 0.0 all-reduce.5.cloned.1.call-start
  6.6 1.1 constant_dynamic-update-slice_fusion.7
  7.7 3.1 %collective-permute-start = (bf16[4,16384]{1,0:T(4,128)(2,1)S(1)}, bf16[4,16384]{1,0:T(4,128)(2,1)S(1)}, u32[]{:S(2)}, u32[]{:S(2)}) collective-permute-start(bf16[4,16384]{1,0:T(4,128)(2,1)S(1)} %get-tuple-element.12), channel_id=1, source_target_pairs={{0,4},{4,8},{8,12},{12,0},{1,5},{5,9},{9,13},{13,1},{2,6},{6,10},{... | collective-permute-start | bytes 393224 | tf_op jit(solution)/shard_map/ppermute | solution.py:26
  10.7 2.1 %collective-permute-start.1 = (bf16[4,16384]{1,0:T(4,128)(2,1)S(1)}, bf16[4,16384]{1,0:T(4,128)(2,1)S(1)}, u32[]{:S(2)}, u32[]{:S(2)}) collective-permute-start(bf16[4,16384]{1,0:T(4,128)(2,1)S(1)} %get-tuple-element.12), channel_id=1, source_target_pairs={{0,12},{4,0},{8,4},{12,8},{1,13},{5,1},{9,5},{13,9},{2,14},{6,2},{... | collective-permute-start | bytes 393224 | tf_op jit(solution)/shard_map/ppermute | solution.py:34
  12.8 0.9 select_reduce_fusion
  13.8 3.3 %collective-permute-done = bf16[4,16384]{1,0:T(4,128)(2,1)S(1)} collective-permute-done((bf16[4,16384]{1,0:T(4,128)(2,1)S(1)}, bf16[4,16384]{1,0:T(4,128)(2,1)S(1)}, u32[]{:S(2)}, u32[]{:S(2)}) %collective-permute-start) | collective-permute-done | bytes 131104 | tf_op jit(solution)/shard_map/ppermute | solution.py:26
  17.1 0.0 collective-permute-start.2
  17.1 0.1 constant_dynamic-update-slice_fusion.6
  17.2 1.3 collective-permute-done.1
  18.5 0.1 constant_dynamic-update-slice_fusion.5
  18.6 5.3 %collective-permute-done.2 = bf16[4,16384]{1,0:T(4,128)(2,1)S(1)} collective-permute-done((bf16[4,16384]{1,0:T(4,128)(2,1)S(1)}, bf16[4,16384]{1,0:T(4,128)(2,1)S(1)}, u32[]{:S(2)}, u32[]{:S(2)}) %collective-permute-start.2) | collective-permute-done | bytes 131104 | tf_op jit(solution)/shard_map/ppermute | solution.py:26
  23.9 0.1 constant_dynamic-update-slice_fusion.4
  23.9 0.2 multiply_reduce_fusion.1
  24.2 0.0 copy-start
  24.2 5.6 %fusion.1 = f32[256,16]{0,1:T(8,128)S(1)} fusion(bf16[16,16384]{1,0:T(8,128)(2,1)S(1)} %constant_dynamic-update-slice_fusion.4, bf16[256,16384]{1,0:T(8,128)(2,1)} %param.4, f32[16]{0:T(128)S(1)} %broadcast_multiply_fusion.1), kind=kOutput, calls=%fused_computation.5 | convolution fusion | flops 134221824 | bytes 8929344 | tf_op jit(solution)/shard_map/fp,mp->fm/dot_general | solution.py:73
  29.9 10.1 %psum.28 = f32[256,16]{0,1:T(8,128)S(1)} all-reduce(f32[256,16]{0,1:T(8,128)S(1)} %fusion.1), channel_id=1, replica_groups=mesh['groups'=2,'frame'=4,'panel'=2,'sub'=2] {'panel','sub'}, use_global_device_ids=true, to_apply=%region_1.2 | all-reduce | flops 4096 | bytes 32768 | tf_op jit(solution)/shard_map/psum | solution.py:76
  40.0 0.1 fusion.3
  40.1 0.1 fusion.5
  40.2 0.2 convert_reduce_fusion.1
  40.4 5.4 %convolution_convert_fusion.1 = bf16[16,16384]{1,0:T(8,128)(2,1)} fusion(bf16[256,16]{0,1:T(8,128)(2,1)S(1)} %get-tuple-element.10, bf16[256,16384]{1,0:T(8,128)(2,1)} %param.4), kind=kOutput, calls=%fused_computation.1 | convolution fusion | flops 134479872 | bytes 8921088 | tf_op jit(solution)/shard_map/fm,fp->mp/dot_general | solution.py:46
  45.8 0.0 all-reduce.5.cloned.1.call-update
  45.8 0.0 all-reduce.7.cloned.1.call-start
  45.9 0.0 copy-done
  45.9 0.6 dynamic-slice
  47.1 10.4 %psum.29 = f32[16]{0:T(128)S(1)} all-reduce(f32[16]{0:T(128)S(1)} %get-tuple-element.9), channel_id=1, replica_groups=mesh['groups'=2,'frame'=4,'panel'=2,'sub'=2] {'frame'}, use_global_device_ids=true, to_apply=%region_7.8 | all-reduce | flops 16 | bytes 128 | tf_op jit(solution)/shard_map/psum | solution.py:78
  57.5 0.1 dynamic-slice_add_fusion.1
  57.6 26.2 %all-reduce.5.cloned.1.call-done = bf16[16,16384]{1,0:T(8,128)(2,1)} async-done(((bf16[16,16384]{1,0:T(8,128)(2,1)}), bf16[16,16384]{1,0:T(8,128)(2,1)}) %all-reduce.5.cloned.1.call-update) | async-done | bytes 524304
  83.8 1.2 constant_dynamic-update-slice_fusion.3
  85.0 1.3 collective-permute-start.3
  86.3 2.6 %collective-permute-start.4 = (bf16[4,16384]{1,0:T(4,128)(2,1)S(1)}, bf16[4,16384]{1,0:T(4,128)(2,1)S(1)}, u32[]{:S(2)}, u32[]{:S(2)}) collective-permute-start(bf16[4,16384]{1,0:T(4,128)(2,1)S(1)} %get-tuple-element.8), channel_id=1, source_target_pairs={{0,12},{4,0},{8,4},{12,8},{1,13},{5,1},{9,5},{13,9},{2,14},{6,2},{... | collective-permute-start | bytes 393224 | tf_op jit(solution)/shard_map/ppermute | solution.py:34
  88.8 3.8 %collective-permute-done.3 = bf16[4,16384]{1,0:T(4,128)(2,1)S(1)} collective-permute-done((bf16[4,16384]{1,0:T(4,128)(2,1)S(1)}, bf16[4,16384]{1,0:T(4,128)(2,1)S(1)}, u32[]{:S(2)}, u32[]{:S(2)}) %collective-permute-start.3) | collective-permute-done | bytes 131104 | tf_op jit(solution)/shard_map/ppermute | solution.py:26
  92.7 0.5 collective-permute-start.5
  93.2 0.1 constant_dynamic-update-slice_fusion.2
  93.3 0.0 collective-permute-done.4
  93.3 0.1 constant_dynamic-update-slice_fusion.1
  93.4 6.1 %collective-permute-done.5 = bf16[4,16384]{1,0:T(4,128)(2,1)S(1)} collective-permute-done((bf16[4,16384]{1,0:T(4,128)(2,1)S(1)}, bf16[4,16384]{1,0:T(4,128)(2,1)S(1)}, u32[]{:S(2)}, u32[]{:S(2)}) %collective-permute-start.5) | collective-permute-done | bytes 131104 | tf_op jit(solution)/shard_map/ppermute | solution.py:26
  99.5 0.1 constant_dynamic-update-slice_fusion
  99.5 0.2 multiply_reduce_fusion
  99.8 5.6 %fusion = f32[256,16]{0,1:T(8,128)S(1)} fusion(bf16[16,16384]{1,0:T(8,128)(2,1)S(1)} %constant_dynamic-update-slice_fusion, bf16[256,16384]{1,0:T(8,128)(2,1)} %param.4, f32[16]{0:T(128)S(1)} %broadcast_multiply_fusion), kind=kOutput, calls=%fused_computation.3 | convolution fusion | flops 134221824 | bytes 8929344 | tf_op jit(solution)/shard_map/fp,mp->fm/dot_general | solution.py:73
  105.4 10.1 %psum.30 = f32[256,16]{0,1:T(8,128)S(1)} all-reduce(f32[256,16]{0,1:T(8,128)S(1)} %fusion), channel_id=1, replica_groups=mesh['groups'=2,'frame'=4,'panel'=2,'sub'=2] {'panel','sub'}, use_global_device_ids=true, to_apply=%region_9.10 | all-reduce | flops 4096 | bytes 32768 | tf_op jit(solution)/shard_map/psum | solution.py:76
  115.6 0.1 fusion.4
  115.7 0.1 fusion.6
  115.8 0.2 convert_reduce_fusion
  115.9 5.4 %convolution_convert_fusion = bf16[16,16384]{1,0:T(8,128)(2,1)} fusion(bf16[256,16]{0,1:T(8,128)(2,1)S(1)} %get-tuple-element.6, bf16[256,16384]{1,0:T(8,128)(2,1)} %param.4), kind=kOutput, calls=%fused_computation | convolution fusion | flops 134479872 | bytes 8921088 | tf_op jit(solution)/shard_map/fm,fp->mp/dot_general | solution.py:46
  121.4 0.0 all-reduce.7.cloned.1.call-update
  121.4 8.9 %psum.31 = f32[16]{0:T(128)S(1)} all-reduce(f32[16]{0:T(128)S(1)} %get-tuple-element.5), channel_id=1, replica_groups=mesh['groups'=2,'frame'=4,'panel'=2,'sub'=2] {'frame'}, use_global_device_ids=true, to_apply=%region_14.15 | all-reduce | flops 16 | bytes 128 | tf_op jit(solution)/shard_map/psum | solution.py:78
  130.3 0.1 dynamic-slice_add_fusion
  130.4 27.9 %all-reduce.7.cloned.1.call-done = bf16[16,16384]{1,0:T(8,128)(2,1)} async-done(((bf16[16,16384]{1,0:T(8,128)(2,1)}), bf16[16,16384]{1,0:T(8,128)(2,1)}) %all-reduce.7.cloned.1.call-update) | async-done | bytes 524304
  158.3 1.8 %add_divide_fusion = f32[4,16384]{1,0:T(4,128)} fusion(bf16[4,16384]{1,0:T(4,128)(2,1)S(1)} %get-tuple-element.8, bf16[16,16384]{1,0:T(8,128)(2,1)} %all-reduce.7.cloned.1.call-done, u32[]{:T(128)S(6)} %multiply.1, f32[4]{0:T(128)S(1)} %dynamic-slice_add_fusion), kind=kLoop, calls=%fused_computation.8 | loop fusion | flops 262144 | bytes 524308 | tf_op jit(solution)/shard_map/div | solution.py:54
  (4 shorter events, 0.1 us)
Async XLA Ops:
  6.5 77.2 %all-reduce.5.cloned.1.call-start = ((), (), s32[]{:S(2)}) async-start(), calls=%async_computation | async-start | bytes 1048576
  7.7 9.4 %collective-permute-start = (bf16[4,16384]{1,0:T(4,128)(2,1)S(1)}, bf16[4,16384]{1,0:T(4,128)(2,1)S(1)}, u32[]{:S(2)}, u32[]{:S(2)}) collective-permute-start(bf16[4,16384]{1,0:T(4,128)(2,1)S(1)} %get-tuple-element.12), channel_id=1, source_target_pairs={{0,4},{4,8},{8,12},{12,0},{1,5},{5,9},{9,13},{13,1},{2,6},{6,10},{... | collective-permute-start | bytes 393224 | tf_op jit(solution)/shard_map/ppermute | solution.py:26
  10.7 7.8 %collective-permute-start.1 = (bf16[4,16384]{1,0:T(4,128)(2,1)S(1)}, bf16[4,16384]{1,0:T(4,128)(2,1)S(1)}, u32[]{:S(2)}, u32[]{:S(2)}) collective-permute-start(bf16[4,16384]{1,0:T(4,128)(2,1)S(1)} %get-tuple-element.12), channel_id=1, source_target_pairs={{0,12},{4,0},{8,4},{12,8},{1,13},{5,1},{9,5},{13,9},{2,14},{6,2},{... | collective-permute-start | bytes 393224 | tf_op jit(solution)/shard_map/ppermute | solution.py:34
  17.1 6.8 %collective-permute-start.2 = (bf16[4,16384]{1,0:T(4,128)(2,1)S(1)}, bf16[4,16384]{1,0:T(4,128)(2,1)S(1)}, u32[]{:S(2)}, u32[]{:S(2)}) collective-permute-start(bf16[4,16384]{1,0:T(4,128)(2,1)S(1)} %collective-permute-done), channel_id=1, source_target_pairs={{0,4},{4,8},{8,12},{12,0},{1,5},{5,9},{9,13},{13,1},{2,6},{6,10},{... | collective-permute-start | bytes 393224 | tf_op jit(solution)/shard_map/ppermute | solution.py:26
  24.2 21.7 %copy-start = (u32[32]{0:T(128)S(1)}, u32[32]{0:T(128)}, u32[]{:S(2)}) copy-start(u32[32]{0:T(128)} %constant.58) | copy-start | bytes 388
  45.8 112.5 %all-reduce.7.cloned.1.call-start = ((), (), s32[]{:S(2)}) async-start(), calls=%async_computation.1 | async-start | bytes 1048576
  85.0 7.7 %collective-permute-start.3 = (bf16[4,16384]{1,0:T(4,128)(2,1)S(1)}, bf16[4,16384]{1,0:T(4,128)(2,1)S(1)}, u32[]{:S(2)}, u32[]{:S(2)}) collective-permute-start(bf16[4,16384]{1,0:T(4,128)(2,1)S(1)} %get-tuple-element.8), channel_id=1, source_target_pairs={{0,4},{4,8},{8,12},{12,0},{1,5},{5,9},{9,13},{13,1},{2,6},{6,10},{... | collective-permute-start | bytes 393224 | tf_op jit(solution)/shard_map/ppermute | solution.py:26
  86.3 7.0 %collective-permute-start.4 = (bf16[4,16384]{1,0:T(4,128)(2,1)S(1)}, bf16[4,16384]{1,0:T(4,128)(2,1)S(1)}, u32[]{:S(2)}, u32[]{:S(2)}) collective-permute-start(bf16[4,16384]{1,0:T(4,128)(2,1)S(1)} %get-tuple-element.8), channel_id=1, source_target_pairs={{0,12},{4,0},{8,4},{12,8},{1,13},{5,1},{9,5},{13,9},{2,14},{6,2},{... | collective-permute-start | bytes 393224 | tf_op jit(solution)/shard_map/ppermute | solution.py:34
  92.7 6.8 %collective-permute-start.5 = (bf16[4,16384]{1,0:T(4,128)(2,1)S(1)}, bf16[4,16384]{1,0:T(4,128)(2,1)S(1)}, u32[]{:S(2)}, u32[]{:S(2)}) collective-permute-start(bf16[4,16384]{1,0:T(4,128)(2,1)S(1)} %collective-permute-done.3), channel_id=1, source_target_pairs={{0,4},{4,8},{8,12},{12,0},{1,5},{5,9},{9,13},{13,1},{2,6},{6,10},{... | collective-permute-start | bytes 393224 | tf_op jit(solution)/shard_map/ppermute | solution.py:26
Sparse Core Ops, SparseCore 0:
  45.9 37.8 all-reduce.4
  121.5 36.7 all-reduce.6
